TPU v7x, 512 devices: a whole 4x8x8 slice. The times are simulated.
512 devices in a mesh: expert: 8 (over x, core), tensor: 64 (over y, z).
Axes of the slice: x: 4, y: 8, z: 8, core: 2. Of those that a mesh axis runs over, the one named last changes fastest.
Arguments:
- tokens: bfloat16 [1536, 6144], P('tensor'), may hold values from -6 to 6
- expert_ids: int32 [1536, 2], P('tensor'), may hold values from 0 to 7, all different within a row; in each aligned block of 24 rows (0 to 23, 24 to 47, ...) at most 12 rows name the same one
- gate_units: int32 [1536, 2], P('tensor'), may hold values from 1 to 65535
- gate_weight: bfloat16 [8, 6144, 8192], P('expert', None, 'tensor'), may hold values from -0.078125 to 0.078125
- up_weight: bfloat16 [8, 6144, 8192], P('expert', None, 'tensor'), may hold values from -0.078125 to 0.078125
- down_weight: bfloat16 [8, 6144, 8192], P('expert', 'tensor'), may hold values from -0.0625 to 0.0625
Outputs:
- expert_mix: bfloat16 [1536, 6144], P('tensor', 'expert')
Inputs may be any that keep to these rules, and one draw needn't show every extreme that they name: `expert_ids`: within each aligned block of 24 rows (the tokens of one tensor index) the two ids of a row differ and no expert is named by more than 12 rows; in every draw some expert is named by exactly 12 rows of some block, and every expert is named somewhere.
All inputs are finite; a program needn't handle non-finite values.
Results may differ from a plain program's by a relative error of at most 0.0057.
Values may be sent and summed in bfloat16 or wider, within the bound.
A program may use at most 128 MiB of HBM per device.

v0:
```python
import jax
import jax.numpy as jnp
from jax import lax
from jax.sharding import PartitionSpec as P


def slot_tables(expert_ids, gate_units, expert_id, capacity):
    tok_rows = expert_ids.shape[0]
    top_count = expert_ids.shape[1]
    flat_route = expert_ids.reshape(-1)
    matches = (flat_route == expert_id).astype(jnp.int32)
    slot_rank = jnp.cumsum(matches) - matches
    slot_ids = jnp.arange(capacity, dtype=jnp.int32)
    assignment = jnp.where(
        (slot_rank[None, :] == slot_ids[:, None]) & (matches[None, :] == 1), 1.0, 0.0
    ).astype(jnp.float32)
    positions = jnp.arange(tok_rows * top_count, dtype=jnp.int32) // top_count
    owners = (positions[:, None] == jnp.arange(tok_rows, dtype=jnp.int32)[None, :]).astype(
        jnp.float32
    )
    unit_vals = gate_units.astype(jnp.float32)
    shares = unit_vals / jnp.sum(unit_vals, axis=1, keepdims=True)
    picker = jnp.dot(
        assignment, owners, precision=lax.Precision.HIGHEST, preferred_element_type=jnp.float32
    )
    weighted = jnp.dot(
        assignment,
        owners * shares.reshape(-1)[:, None],
        precision=lax.Precision.HIGHEST,
        preferred_element_type=jnp.float32,
    )
    return (picker, weighted)


def local(tokens, expert_ids, gate_units, gate_weight, up_weight, down_weight):
    experts = lax.axis_size("expert")
    expert_id = lax.axis_index("expert")
    tok_rows = tokens.shape[0]
    capacity = min(tok_rows, 4 * tok_rows // experts)
    picker, weighted = slot_tables(expert_ids, gate_units, expert_id, capacity)
    picked = jnp.dot(
        picker.astype(jnp.bfloat16), tokens, preferred_element_type=jnp.float32
    ).astype(jnp.bfloat16)
    w_gate = gate_weight[0]
    w_up = up_weight[0]
    w_down = down_weight[0]
    shard_piece = lax.all_gather(picked, "tensor", axis=0, tiled=True)
    gate_vals = jnp.dot(shard_piece, w_gate, preferred_element_type=jnp.float32)
    up_vals = jnp.dot(shard_piece, w_up, preferred_element_type=jnp.float32)
    hidden = (jax.nn.silu(gate_vals) * up_vals).astype(jnp.bfloat16)
    gathered = lax.all_gather(hidden, "tensor", axis=1, tiled=True)
    projected = lax.dot_general(
        gathered, w_down, (((1,), (1,)), ((), ())), preferred_element_type=jnp.float32
    )
    outputs = projected.astype(jnp.bfloat16)
    returned = lax.all_to_all(outputs, "tensor", split_axis=0, concat_axis=1, tiled=True)
    contribution = lax.dot_general(
        weighted,
        returned.astype(jnp.float32),
        (((0,), (0,)), ((), ())),
        precision=lax.Precision.HIGHEST,
        preferred_element_type=jnp.float32,
    )
    summed_all = lax.psum(contribution, "expert")
    col_width = contribution.shape[1] // experts
    mixed = lax.dynamic_slice_in_dim(summed_all, expert_id * col_width, col_width, 1)
    return mixed.astype(jnp.bfloat16)


def solution(mesh):
    return jax.shard_map(
        local,
        mesh=mesh,
        in_specs=(
            P("tensor", None),
            P("tensor", None),
            P("tensor", None),
            P("expert", None, "tensor"),
            P("expert", None, "tensor"),
            P("expert", "tensor", None),
        ),
        out_specs=P("tensor", "expert"),
        check_vma=False,
    )
```

profile of v0, /device:TPU:8, one launch (start us, length us, event | category | flops | bytes accessed | tf_op | source)
XLA Modules:
  0.0 349.5 jit_solution(7697855502720402069)
XLA Ops:
  6.5 0.0 copy-start
  6.5 0.8 compare_convert_fusion
  7.3 0.1 copy.17
  7.4 0.1 reshape.76
  7.5 0.1 reshape.79
  7.6 0.1 reduce-window.8
  7.7 0.1 reduce
  7.8 0.2 convolution_convert_fusion.1
  8.0 1.8 fusion
  9.9 0.0 all-gather.6.cloned.1.call-update
  9.9 0.0 all-gather.4.cloned.1.call-start
  9.9 124.4 %all-gather.6.cloned.1.call-done = bf16[64,12,6144]{2,1,0:T(8,128)(2,1)} async-done(((bf16[1,12,6144]{2,1,0:T(8,128)(2,1)}), bf16[64,12,6144]{2,1,0:T(8,128)(2,1)}) %all-gather.6.cloned.1.call-update) | async-done | bytes 9437200 | tf_op jit(solution)/shard_map/all_gather | solution.py:47
  134.3 13.7 %reshape.78 = bf16[768,6144]{1,0:T(8,128)(2,1)} reshape(bf16[64,12,6144]{2,1,0:T(8,128)(2,1)} %all-gather.6.cloned.1.call-done) | data formatting | bytes 18874368
  148.1 6.1 %fusion.5 = f32[768,128]{1,0:T(8,128)S(1)} fusion(bf16[768,6144]{1,0:T(8,128)(2,1)} %reshape.78, bf16[1,6144,128]{2,1,0:T(8,128)(2,1)S(1)} %copy-done), kind=kOutput, calls=%fused_computation.6 | convolution fusion | flops 1207959552 | bytes 11403264 | tf_op jit(solution)/shard_map/dot_general | solution.py:48
  154.2 0.3 copy-done.1
  154.5 0.4 copy-done.4
  155.0 3.3 fusion.10
  158.2 0.0 all-gather.4.cloned.1.call-update
  158.3 124.2 %all-gather.4.cloned.1.call-done = bf16[768,8192]{1,0:T(8,128)(2,1)} async-done(((bf16[768,128]{1,0:T(8,128)(2,1)}), bf16[768,8192]{1,0:T(8,128)(2,1)}) %all-gather.4.cloned.1.call-update) | async-done | bytes 12582928 | tf_op jit(solution)/shard_map/all_gather | solution.py:51
  282.5 8.6 %fusion.13 = bf16[768,96]{0,1:T(8,128)(2,1)S(1)} fusion(bf16[768,8192]{1,0:T(8,128)(2,1)} %all-gather.4.cloned.1.call-done, bf16[1,96,8192]{2,1,0:T(8,128)(2,1)S(1)} %copy-done.2), kind=kOutput, calls=%fused_computation.10 | convolution fusion | flops 1208033280 | bytes 14303232 | tf_op jit(solution)/shard_map/dot_general | solution.py:52
  291.1 0.2 copy.21
  291.3 0.8 all_to_all.14
  292.0 7.8 %all-to-all-start = ((bf16[64,12,96]{2,1,0:T(8,128)(2,1)}), bf16[64,12,96]{2,1,0:T(8,128)(2,1)S(1)}, u32[]{:S(2)}, u32[]{:S(2)}) async-start(bf16[64,12,96]{2,1,0:T(8,128)(2,1)} %all_to_all.14), calls=%async_computation | async-start | bytes 524288 | tf_op jit(solution)/shard_map/all_to_all | solution.py:56
  299.8 0.1 copy.20
  299.9 0.1 mul.20
  300.0 0.2 fusion.16
  300.2 12.0 %all-to-all-done = bf16[64,12,96]{2,1,0:T(8,128)(2,1)S(1)} async-done(((bf16[64,12,96]{2,1,0:T(8,128)(2,1)}), bf16[64,12,96]{2,1,0:T(8,128)(2,1)S(1)}, u32[]{:S(2)}, u32[]{:S(2)}) %all-to-all-start) | async-done | bytes 147488 | tf_op jit(solution)/shard_map/all_to_all | solution.py:56
  312.2 0.1 copy.22
  312.2 0.3 all_to_all.17
  312.5 0.4 fusion.39
  313.0 29.1 %all-reduce.1 = bf16[24,6144]{1,0:T(8,128)(2,1)S(1)} all-reduce(f32[24,6144]{1,0:T(8,128)S(1)} %fusion.39), channel_id=1, replica_groups=mesh['expert'=8,'tensor'=64] {'expert'}, use_global_device_ids=true, to_apply=%region_2.3 | all-reduce | flops 147456 | bytes 884736 | tf_op jit(solution)/shard_map/psum | solution.py:64
  342.0 0.6 dynamic-slice_convert_fusion
  (13 shorter events, 0.1 us)
Async XLA Ops:
  6.5 141.6 %copy-start = (bf16[1,6144,128]{2,1,0:T(8,128)(2,1)S(1)}, bf16[1,6144,128]{2,1,0:T(8,128)(2,1)}, u32[]{:S(2)}) copy-start(bf16[1,6144,128]{2,1,0:T(8,128)(2,1)} %param.9) | copy-start | bytes 4718596
  6.5 127.8 %all-gather.6.cloned.1.call-start = ((), (), s32[]{:S(2)}) async-start(), calls=%async_computation.2 | async-start | bytes 12779520 | tf_op jit(solution)/shard_map/all_gather | solution.py:47
  9.9 272.6 %all-gather.4.cloned.1.call-start = ((), (), s32[]{:S(2)}) async-start(), calls=%async_computation.1 | async-start | bytes 12779520 | tf_op jit(solution)/shard_map/all_gather | solution.py:51
  148.1 6.4 %copy-start.1 = (bf16[768,6144]{1,0:T(8,128)(2,1)S(1)}, bf16[768,6144]{1,0:T(8,128)(2,1)}, u32[]{:S(2)}) copy-start(bf16[768,6144]{1,0:T(8,128)(2,1)} %reshape.78) | copy-start | bytes 28311556
  148.1 6.9 %copy-start.4 = (bf16[1,6144,128]{2,1,0:T(8,128)(2,1)S(1)}, bf16[1,6144,128]{2,1,0:T(8,128)(2,1)}, u32[]{:S(2)}) copy-start(bf16[1,6144,128]{2,1,0:T(8,128)(2,1)} %param.10) | copy-start | bytes 4718596
  154.9 3.3 copy-start.3
  154.9 127.6 %copy-start.2 = (bf16[1,96,8192]{2,1,0:T(8,128)(2,1)S(1)}, bf16[1,96,8192]{2,1,0:T(8,128)(2,1)}, u32[]{:S(2)}) copy-start(bf16[1,96,8192]{2,1,0:T(8,128)(2,1)} %param.11) | copy-start | bytes 4718596
  292.0 20.1 %all-to-all-start = ((bf16[64,12,96]{2,1,0:T(8,128)(2,1)}), bf16[64,12,96]{2,1,0:T(8,128)(2,1)S(1)}, u32[]{:S(2)}, u32[]{:S(2)}) async-start(bf16[64,12,96]{2,1,0:T(8,128)(2,1)} %all_to_all.14), calls=%async_computation | async-start | bytes 524288 | tf_op jit(solution)/shard_map/all_to_all | solution.py:56
Sparse Core Ops, SparseCore 0:
  10.4 123.9 all-gather.5
  158.4 124.1 all-gather.3
where the time goes:
time: 350 us
  waiting for transfers between devices  261 us (75%)
  blocking collectives  29.1 us (8%)
  matrix products  20.7 us (6%)
  local copies, waits for them, and re-layouts  16.8 us (5%)
  between operations  13.5 us (4%)
  starting transfers between devices  7.81 us (2%)
    all_gather x1, waiting for transfers between devices, local(): shard_piece = lax.all_gather(picked, 'tensor', axis=0, tiled=True)  124 us
    all_gather x1, waiting for transfers between devices, local(): gathered = lax.all_gather(hidden, 'tensor', axis=1, tiled=True)  124 us
    psum x1, blocking collectives, local(): summed_all = lax.psum(contribution, 'expert')  29.1 us
    unnamed x11, local copies, waits for them, and re-layouts  14.5 us
    all_to_all x1, waiting for transfers between devices, local(): lax.all_to_all(outputs, 'tensor', split_axis=0, concat_axis=1, tiled=True)  12 us
    dot_general x1, matrix products, local(): lax.dot_general(gathered, w_down, (((1,), (1,)), ((), ())), preferred_ele...  8.57 us
    all_to_all x1, starting transfers between devices, local(): lax.all_to_all(outputs, 'tensor', split_axis=0, concat_axis=1, tiled=True)  7.77 us
  transfers between devices with their start and end apart: 3, of which 3 were waited for; matrix products, arithmetic and copies ran while one was open for 0% of the time, Pallas kernels for 0%

commit v1 on v0

--- a/solution.py
+++ b/solution.py
@@ -44,7 +44,9 @@
     w_gate = gate_weight[0]
     w_up = up_weight[0]
     w_down = down_weight[0]
-    shard_piece = lax.all_gather(picked, "tensor", axis=0, tiled=True)
+    shard_piece = jnp.concatenate(
+        lax.all_to_all(jnp.stack([picked] * lax.axis_size("tensor")), "tensor", 0, 0), axis=0
+    )
     gate_vals = jnp.dot(shard_piece, w_gate, preferred_element_type=jnp.float32)
     up_vals = jnp.dot(shard_piece, w_up, preferred_element_type=jnp.float32)
     hidden = (jax.nn.silu(gate_vals) * up_vals).astype(jnp.bfloat16)

time: 350 us -> 591 us (1.69)
  blocking collectives: 29.1 us -> 351 us
  waiting for transfers between devices: 261 us -> 174 us
  local copies, waits for them, and re-layouts: 16.8 us -> 22.8 us
    all_to_all x0 -> x1, blocking collectives: none -> 322 us  [local(): lax.all_to_all(jnp.stack([picked] * lax.axis_size('tensor')), 'tensor', 0...]
    all_gather x1 -> x0, waiting for transfers between devices: 124 us -> none  [local(): shard_piece = lax.all_gather(picked, 'tensor', axis=0, tiled=True)]
    all_gather x1, waiting for transfers between devices: 124 us -> 162 us  [local(): gathered = lax.all_gather(hidden, 'tensor', axis=1, tiled=True)]
    unnamed x11 -> x10, local copies, waits for them, and re-layouts: 14.5 us -> 0.71 us
    reshape x0 -> x1, local copies, waits for them, and re-layouts: none -> 13.7 us  [local(): jnp.concatenate(lax.all_to_all(jnp.stack([picked] * lax.axis_size('tensor...]
    another operation x0 -> x1, local copies, waits for them, and re-layouts: none -> 6.04 us  [local(): jnp.stack([picked] * lax.axis_size('tensor'))]
  transfers between devices with their start and end apart: 3 -> 2, of which waited for: 3 -> 2; matrix products, arithmetic and copies ran while one was open for 0% -> 0% of each run, Pallas kernels for 0% -> 0%
where the time goes in v1:
time: 591 us; the launch traced here: 590 us
  blocking collectives  351 us (59%)
  waiting for transfers between devices  174 us (29%)
  local copies, waits for them, and re-layouts  22.8 us (4%)
  matrix products  20 us (3%)
  between operations  13.5 us (2%)
  starting transfers between devices  7.77 us (1%)
    all_to_all x1, blocking collectives, local(): lax.all_to_all(jnp.stack([picked] * lax.axis_size('tensor')), 'tensor', 0...  322 us
    all_gather x1, waiting for transfers between devices, local(): gathered = lax.all_gather(hidden, 'tensor', axis=1, tiled=True)  162 us
    psum x1, blocking collectives, local(): summed_all = lax.psum(contribution, 'expert')  29.1 us
    reshape x1, local copies, waits for them, and re-layouts, local(): jnp.concatenate(lax.all_to_all(jnp.stack([picked] * lax.axis_size('tensor...  13.7 us
    all_to_all x1, waiting for transfers between devices, local(): lax.all_to_all(outputs, 'tensor', split_axis=0, concat_axis=1, tiled=True)  12 us
  transfers between devices with their start and end apart: 2, of which 2 were waited for; matrix products, arithmetic and copies ran while one was open for 0% of the time, Pallas kernels for 0%

profile of v1, /device:TPU:8, one launch (start us, length us, event | category | flops | bytes accessed | tf_op | source)
XLA Modules:
  0.0 589.9 jit_solution(12311861562303446101)
XLA Ops:
  6.5 0.8 compare_convert_fusion
  7.3 0.1 copy.11
  7.4 0.1 reshape.82
  7.5 0.1 reshape.83
  7.6 0.1 reduce-window.8
  7.7 0.1 reduce
  7.8 0.2 convolution_convert_fusion.1
  8.0 1.2 convolution_convert_fusion
  9.2 6.0 %stack.2 = bf16[64,12,6144]{2,1,0:T(8,128)(2,1)} broadcast(bf16[12,6144]{1,0:T(8,128)(2,1)S(1)} %convolution_convert_fusion), dimensions={1,2} | broadcast | bytes 9584640 | tf_op jit(solution)/shard_map/stack | solution.py:48
  15.2 321.8 %all_to_all.24 = bf16[64,12,6144]{2,1,0:T(8,128)(2,1)} all-to-all(bf16[64,12,6144]{2,1,0:T(8,128)(2,1)} %stack.2), channel_id=1, replica_groups=mesh['expert'=8,'tensor'=64] {'tensor'}, dimensions={0} | all-to-all | bytes 18874368 | tf_op jit(solution)/shard_map/all_to_all | solution.py:48
  337.0 13.7 %reshape.80 = bf16[768,6144]{1,0:T(8,128)(2,1)} reshape(bf16[64,12,6144]{2,1,0:T(8,128)(2,1)} %all_to_all.24) | data formatting | bytes 18874368 | tf_op jit(solution)/shard_map/reshape | solution.py:47
  350.8 6.1 %fusion.4 = f32[768,128]{1,0:T(8,128)S(1)} fusion(bf16[768,6144]{1,0:T(8,128)(2,1)} %reshape.80, bf16[1,6144,128]{2,1,0:T(8,128)(2,1)S(1)} %copy-done), kind=kOutput, calls=%fused_computation.5 | convolution fusion | flops 1207959552 | bytes 11403264 | tf_op jit(solution)/shard_map/dot_general | solution.py:50
  356.9 0.3 copy-done.1
  357.2 0.4 copy-done.4
  357.6 3.3 fusion.9
  360.9 0.0 all-gather.2.cloned.1.call-update
  360.9 0.0 copy-done.3
  360.9 162.0 %all-gather.2.cloned.1.call-done = bf16[768,8192]{1,0:T(8,128)(2,1)} async-done(((bf16[768,128]{1,0:T(8,128)(2,1)}), bf16[768,8192]{1,0:T(8,128)(2,1)}) %all-gather.2.cloned.1.call-update) | async-done | bytes 12582928 | tf_op jit(solution)/shard_map/all_gather | solution.py:53
  522.9 0.0 copy-done.2
  522.9 8.6 %fusion.12 = bf16[768,96]{0,1:T(8,128)(2,1)S(1)} fusion(bf16[768,8192]{1,0:T(8,128)(2,1)} %all-gather.2.cloned.1.call-done, bf16[1,96,8192]{2,1,0:T(8,128)(2,1)S(1)} %copy-done.2), kind=kOutput, calls=%fused_computation.9 | convolution fusion | flops 1208033280 | bytes 14303232 | tf_op jit(solution)/shard_map/dot_general | solution.py:54
  531.5 0.2 copy.15
  531.7 0.8 all_to_all.18
  532.4 7.8 %all-to-all-start.1 = ((bf16[64,12,96]{2,1,0:T(8,128)(2,1)}), bf16[64,12,96]{2,1,0:T(8,128)(2,1)S(1)}, u32[]{:S(2)}, u32[]{:S(2)}) async-start(bf16[64,12,96]{2,1,0:T(8,128)(2,1)} %all_to_all.18), calls=%async_computation.1 | async-start | bytes 524288 | tf_op jit(solution)/shard_map/all_to_all | solution.py:58
  540.2 0.1 copy.14
  540.3 0.1 mul.20
  540.4 0.2 fusion.15
  540.6 12.0 %all-to-all-done.1 = bf16[64,12,96]{2,1,0:T(8,128)(2,1)S(1)} async-done(((bf16[64,12,96]{2,1,0:T(8,128)(2,1)}), bf16[64,12,96]{2,1,0:T(8,128)(2,1)S(1)}, u32[]{:S(2)}, u32[]{:S(2)}) %all-to-all-start.1) | async-done | bytes 147488 | tf_op jit(solution)/shard_map/all_to_all | solution.py:58
  552.6 0.1 copy.16
  552.6 0.3 all_to_all.21
  552.9 0.4 fusion.38
  553.4 29.1 %all-reduce.1 = bf16[24,6144]{1,0:T(8,128)(2,1)S(1)} all-reduce(f32[24,6144]{1,0:T(8,128)S(1)} %fusion.38), channel_id=1, replica_groups=mesh['expert'=8,'tensor'=64] {'expert'}, use_global_device_ids=true, to_apply=%region_2.3 | all-reduce | flops 147456 | bytes 884736 | tf_op jit(solution)/shard_map/psum | solution.py:66
  582.5 0.6 dynamic-slice_convert_fusion
  (12 shorter events, 0.1 us)
Async XLA Ops:
  6.5 344.2 %copy-start = (bf16[1,6144,128]{2,1,0:T(8,128)(2,1)S(1)}, bf16[1,6144,128]{2,1,0:T(8,128)(2,1)}, u32[]{:S(2)}) copy-start(bf16[1,6144,128]{2,1,0:T(8,128)(2,1)} %param.9) | copy-start | bytes 4718596
  6.5 516.4 %all-gather.2.cloned.1.call-start = ((), (), s32[]{:S(2)}) async-start(), calls=%async_computation.2 | async-start | bytes 12779520 | tf_op jit(solution)/shard_map/all_gather | solution.py:53
  350.8 6.4 %copy-start.1 = (bf16[768,6144]{1,0:T(8,128)(2,1)S(1)}, bf16[768,6144]{1,0:T(8,128)(2,1)}, u32[]{:S(2)}) copy-start(bf16[768,6144]{1,0:T(8,128)(2,1)} %reshape.80) | copy-start | bytes 28311556
  350.8 6.9 %copy-start.4 = (bf16[1,6144,128]{2,1,0:T(8,128)(2,1)S(1)}, bf16[1,6144,128]{2,1,0:T(8,128)(2,1)}, u32[]{:S(2)}) copy-start(bf16[1,6144,128]{2,1,0:T(8,128)(2,1)} %param.10) | copy-start | bytes 4718596
  357.6 3.3 copy-start.3
  357.6 165.3 %copy-start.2 = (bf16[1,96,8192]{2,1,0:T(8,128)(2,1)S(1)}, bf16[1,96,8192]{2,1,0:T(8,128)(2,1)}, u32[]{:S(2)}) copy-start(bf16[1,96,8192]{2,1,0:T(8,128)(2,1)} %param.11) | copy-start | bytes 4718596
  532.4 20.1 %all-to-all-start.1 = ((bf16[64,12,96]{2,1,0:T(8,128)(2,1)}), bf16[64,12,96]{2,1,0:T(8,128)(2,1)S(1)}, u32[]{:S(2)}, u32[]{:S(2)}) async-start(bf16[64,12,96]{2,1,0:T(8,128)(2,1)} %all_to_all.18), calls=%async_computation.1 | async-start | bytes 524288 | tf_op jit(solution)/shard_map/all_to_all | solution.py:58
Sparse Core Ops, SparseCore 0:
  361.0 161.8 all-gather.1
